TPU v7x, 128 devices: a whole 4x4x4 slice. The times are simulated.
128 devices in a mesh: dp: 64 (over z, y, x), expert: 2 (over core).
Axes of the slice: x: 4, y: 4, z: 4, core: 2. Of those that a mesh axis runs over, the one named last changes fastest.
Arguments:
- hidden: bfloat16 [2, 65536, 1024], P('expert', 'dp'), may hold values from -6 to 6
- cotangent: bfloat16 [2, 65536, 3584], P('expert', 'dp'), may hold values from -6 to 6
- counts: int32 [2, 64], P('expert', 'dp'), may hold values from 1 to 1024, as said below
- placement: int32 [2, 4], replicated, may hold values from 0 to 1, as said below
- weight: bfloat16 [2, 1024, 3584], P('expert', 'dp'), may hold values from -4 to 4
- moment: float32 [2, 1024, 3584], P('expert', 'dp'), may hold values from -2 to 2
- second: float32 [2, 1024, 3584], P('expert', 'dp'), may hold values from 0.005 to 1
- serving: bfloat16 [2, 4, 1024, 3584], P('expert', None, 'dp'), may hold values from -4 to 4
Outputs:
- d_hidden: bfloat16 [2, 65536, 1024], P('expert', 'dp')
- new_weight: bfloat16 [2, 1024, 3584], P('expert', 'dp')
- new_moment: float32 [2, 1024, 3584], P('expert', 'dp')
- new_second: float32 [2, 1024, 3584], P('expert', 'dp')
- served: bfloat16 [2, 4, 1024, 3584], P('expert', None, 'dp')
Inputs may be any that keep to these rules, and one draw needn't show every extreme that they name: `counts`: every count is reached by some expert and data shard in every draw at its upper end, 1024. `placement`: some two groups hold different experts as their first replica.
All inputs are finite; a program needn't handle non-finite values.
Results may differ from a plain program's by a relative error of at most 0.0012.
Values may be sent and summed in bfloat16 or wider, within the bound.
A program may use at most 128 MiB of HBM per device.

v0:
```python
import jax
import jax.numpy as jnp
from jax import lax
from jax.sharding import Mesh
from jax.sharding import PartitionSpec as P

D = 3584
DP = ("dp_0", "dp_1", "dp_2")
beta_one = 0.9
beta_two = 0.95
bias_one = 1.0 - 0.9**20
bias_two = 1.0 - 0.95**20
learn_rate = 0.05
decay_rate = 0.1
epsilon = 1e-08


def summed_rows(array, axes, dim):
    if not axes:
        return array
    nearer = lax.psum_scatter(array, axes[0], scatter_dimension=dim, tiled=True)
    return summed_rows(nearer, axes[1:], dim)


def on_device(hidden, cotangent, counts, placement, weight, moment, second, serving):
    scale = D ** (-0.5)
    acts = hidden[0]
    grads_out = cotangent[0]
    matrix = weight[0]
    tokens = acts.shape[0]
    owned = matrix.shape[0]
    width = matrix.shape[1]
    live = jnp.arange(tokens, dtype=jnp.int32) < counts[0, 0]
    masked = jnp.where(live[:, None], grads_out, jnp.zeros_like(grads_out))
    d_full = scale * jnp.dot(
        masked, lax.all_gather(matrix, DP, axis=0, tiled=True).T, preferred_element_type=jnp.float32
    )
    d_hid = d_full.astype(jnp.bfloat16)
    full_term = scale * jnp.dot(acts.T, masked, preferred_element_type=jnp.float32)
    grad = summed_rows(full_term, DP, 0)
    first_new = beta_one * moment[0] + (1.0 - beta_one) * grad
    squares_new = beta_two * second[0] + (1.0 - beta_two) * grad * grad
    step = first_new / bias_one / (jnp.sqrt(squares_new / bias_two) + epsilon)
    current = matrix.astype(jnp.float32)
    updated = current - learn_rate * (step + decay_rate * current)
    delta = (updated - current).astype(jnp.bfloat16)
    groups = lax.axis_size("expert")
    flat = delta.reshape(groups, -1)
    spread = lax.all_to_all(flat, "expert", split_axis=0, concat_axis=0, tiled=True)
    chosen = jnp.take(spread, placement.T, axis=0)
    arrived = lax.all_to_all(chosen, "expert", split_axis=1, concat_axis=1, tiled=True)
    copies = arrived.shape[0]
    incoming = arrived.reshape(copies, owned, width)
    served = (serving[0].astype(jnp.float32) + incoming.astype(jnp.float32)).astype(jnp.bfloat16)
    return (
        d_hid[None],
        updated.astype(jnp.bfloat16)[None],
        first_new[None],
        squares_new[None],
        served[None],
    )


def solution(mesh):
    torus = Mesh(
        mesh.devices.reshape(4, 4, 4, mesh.shape["expert"]), ("dp_0", "dp_1", "dp_2", "expert")
    )
    return jax.shard_map(
        on_device,
        mesh=torus,
        in_specs=(
            P("expert", DP, None),
            P("expert", DP, None),
            P("expert", DP),
            P(),
            P("expert", DP, None),
            P("expert", DP, None),
            P("expert", DP, None),
            P("expert", None, DP, None),
        ),
        out_specs=(
            P("expert", DP, None),
            P("expert", DP, None),
            P("expert", DP, None),
            P("expert", DP, None),
            P("expert", None, DP, None),
        ),
        check_vma=False,
    )
```

profile of v0, /device:TPU:1, one launch (start us, length us, event | category | flops | bytes accessed | tf_op | source)
XLA Modules:
  0.0 302.0 jit_solution(9500016079672712635)
XLA Ops:
  8.0 0.0 copy-start
  8.0 0.0 reduce-scatter.8.cloned.1.call-start
  8.9 0.8 copy-done
  9.6 14.4 %multiply_bitcast_fusion = f32[1024,3584]{0,1:T(8,128)} fusion(bf16[1,1024,3584]{2,1,0:T(8,128)(2,1)} %param.9, pred[1024]{0:T(1024)(128)(4,1)S(1)} %iota_compare_fusion, bf16[1,1024,1024]{2,1,0:T(8,128)(2,1)S(1)} %copy-done), kind=kOutput, calls=%fused_computation.1 | convolution fusion | flops 7523532800 | bytes 24118272 | tf_op jit(solution)/shard_map/dot_general | solution.py:39
  24.0 0.0 reduce-scatter.8.cloned.1.call-update
  24.0 0.0 copy-start.4
  24.0 0.0 reduce-scatter.10.cloned.1.call-start
  24.1 135.1 %reduce-scatter.8.cloned.1.call-done = f32[256,3584]{0,1:T(8,128)} async-done(((f32[1024,3584]{0,1:T(8,128)}), f32[256,3584]{0,1:T(8,128)}) %reduce-scatter.8.cloned.1.call-update) | async-done | bytes 3670032 | tf_op jit(solution)/shard_map/reduce_scatter | solution.py:21
  159.1 5.2 %copy.58 = f32[256,3584]{1,0:T(8,128)} copy(f32[256,3584]{0,1:T(8,128)} %reduce-scatter.8.cloned.1.call-done) | data formatting | bytes 7340032
  164.3 0.0 reduce-scatter.10.cloned.1.call-update
  164.3 0.0 all-gather.3.cloned.1.call-start
  164.4 0.5 all-gather.3.cloned.1.call-update
  164.9 0.0 reduce-scatter.12.cloned.1.call-start
  165.0 0.0 copy-done.4
  165.0 0.1 copy.55
  165.1 0.1 reshape.51
  165.2 42.3 %reduce-scatter.10.cloned.1.call-done = f32[64,3584]{1,0:T(8,128)} async-done(((f32[256,3584]{1,0:T(8,128)}), f32[64,3584]{1,0:T(8,128)}) %reduce-scatter.10.cloned.1.call-update) | async-done | bytes 917520
  207.4 0.0 reduce-scatter.12.cloned.1.call-update
  207.5 0.0 copy-start.1
  207.5 0.0 copy-start.2
  207.5 0.0 copy-start.3
  207.5 54.5 %all-gather.3.cloned.1.call-done = bf16[1,1024,3584]{2,1,0:T(8,128)(2,1)} async-done(((bf16[1,16,3584]{2,1,0:T(8,128)(2,1)}), bf16[1,1024,3584]{2,1,0:T(8,128)(2,1)}) %all-gather.3.cloned.1.call-update) | async-done | bytes 7340048 | tf_op jit(solution)/shard_map/all_gather | solution.py:36
  262.0 13.2 %fusion.11 = bf16[1,1024,1024]{2,1,0:T(8,128)(2,1)} fusion(bf16[1,1024,3584]{2,1,0:T(8,128)(2,1)} %all-gather.3.cloned.1.call-done, bf16[1,1024,3584]{2,1,0:T(8,128)(2,1)} %param.9, pred[1024]{0:T(1024)(128)(4,1)S(1)} %iota_compare_fusion), kind=kOutput, calls=%fused_computation.13 | convolution fusion | flops 7521959936 | bytes 16778240 | tf_op jit(solution)/shard_map/dot_general | solution.py:35
  275.2 0.0 reduce-scatter.12.cloned.1.call-done
  275.2 0.0 copy-done.1
  275.2 0.0 copy-done.2
  275.2 0.0 copy-done.3
  275.2 1.9 fusion.17
  277.1 0.1 all_to_all.15
  277.1 0.5 broadcast.53
  277.7 1.4 reduce
  279.1 0.1 reshape.65
  279.2 4.3 %all_to_all.18 = bf16[2,2,14336]{2,1,0:T(2,128)(2,1)S(1)} all-to-all(bf16[2,2,14336]{2,1,0:T(2,128)(2,1)S(1)} %reshape.65), channel_id=1, replica_groups=mesh['dp_0'=4,'dp_1'=4,'dp_2'=4,'expert'=2] {'expert'}, dimensions={0} | all-to-all | bytes 229376 | tf_op jit(solution)/shard_map/all_to_all | solution.py:49
  283.4 0.1 reshape.66
  283.6 0.2 copy.65
  283.7 0.8 gather_fusion
  284.6 0.3 reshape.50
  284.9 0.6 copy_select_fusion
  285.5 4.1 %all_to_all.19 = bf16[4,2,28672]{2,0,1:T(4,128)(2,1)S(1)} all-to-all(bf16[4,2,28672]{2,0,1:T(4,128)(2,1)S(1)} %copy_select_fusion), channel_id=1, replica_groups=mesh['dp_0'=4,'dp_1'=4,'dp_2'=4,'expert'=2] {'expert'}, dimensions={1} | all-to-all | bytes 917504 | tf_op jit(solution)/shard_map/all_to_all | solution.py:51
  289.6 1.4 copy.57
  291.0 2.0 reshape.48
  293.0 1.9 add_convert_fusion
  (4 shorter events, 0.0 us)
Async XLA Ops:
  8.0 1.6 copy-start
  8.0 151.1 %reduce-scatter.8.cloned.1.call-start = ((), (), s32[]{:S(2)}) async-start(), calls=%async_computation.5 | async-start | bytes 18350080 | tf_op jit(solution)/shard_map/reduce_scatter | solution.py:21
  24.0 140.9 %copy-start.4 = (s32[2,4]{1,0:T(2,128)S(1)}, s32[2,4]{1,0:T(2,128)}, u32[]{:S(2)}) copy-start(s32[2,4]{1,0:T(2,128)} %param.11) | copy-start | bytes 100
  24.0 183.4 %reduce-scatter.10.cloned.1.call-start = ((), (), s32[]{:S(2)}) async-start(), calls=%async_computation.7 | async-start | bytes 4587520
  164.3 97.7 %all-gather.3.cloned.1.call-start = ((), (), s32[]{:S(2)}) async-start(), calls=%async_computation.6 | async-start | bytes 7454720 | tf_op jit(solution)/shard_map/all_gather | solution.py:36
  164.9 110.3 %reduce-scatter.12.cloned.1.call-start = ((), (), s32[]{:S(2)}) async-start(), calls=%async_computation.8 | async-start | bytes 1146880 | tf_op jit(solution)/shard_map/reduce_scatter | solution.py:21
  207.5 67.7 %copy-start.1 = (bf16[1,16,3584]{2,1,0:T(8,128)(2,1)S(1)}, bf16[1,16,3584]{2,1,0:T(8,128)(2,1)}, u32[]{:S(2)}) copy-start(bf16[1,16,3584]{2,1,0:T(8,128)(2,1)} %param.12) | copy-start | bytes 344068
  207.5 67.7 %copy-start.2 = (f32[1,16,3584]{2,1,0:T(8,128)S(1)}, f32[1,16,3584]{2,1,0:T(8,128)}, u32[]{:S(2)}) copy-start(f32[1,16,3584]{2,1,0:T(8,128)} %param.14) | copy-start | bytes 688132
  207.5 67.7 %copy-start.3 = (f32[1,16,3584]{2,1,0:T(8,128)S(1)}, f32[1,16,3584]{2,1,0:T(8,128)}, u32[]{:S(2)}) copy-start(f32[1,16,3584]{2,1,0:T(8,128)} %param.13) | copy-start | bytes 688132
Sparse Core Ops, SparseCore 0:
  24.1 134.9 reduce-scatter.7
  164.5 42.9 reduce-scatter.9
  209.9 22.5 reduce-scatter.11
Sparse Core Ops, SparseCore 1:
  167.6 94.4 all-gather.2
where the time goes:
time: 302 us
  waiting for transfers between devices  232 us (77%)
  matrix products  27.6 us (9%)
  between operations  16.1 us (5%)
  local copies, waits for them, and re-layouts  11.6 us (4%)
  blocking collectives  8.34 us (3%)
  other arithmetic  5.8 us (2%)
    reduce_scatter x2, waiting for transfers between devices, summed_rows(): nearer = lax.psum_scatter(array, axes[0], scatter_dimension=dim, tiled=True)  135 us
    all_gather x1, waiting for transfers between devices, on_device(): lax.all_gather(matrix, DP, axis=0, tiled=True)  54.5 us
    unnamed x5, waiting for transfers between devices  42.8 us
    dot_general x1, matrix products, on_device(): jnp.dot(acts.T, masked, preferred_element_type=jnp.float32)  14.4 us
    dot_general x1, matrix products, on_device(): jnp.dot(masked, lax.all_gather(matrix, DP, axis=0, tiled=True).T, preferr...  13.2 us
    unnamed x14, local copies, waits for them, and re-layouts  6.33 us
  transfers between devices with their start and end apart: 4, of which 3 were waited for; matrix products, arithmetic and copies ran while one was open for 4% of the time, Pallas kernels for 0%

commit v1 on v0

--- a/solution.py
+++ b/solution.py
@@ -33,7 +33,11 @@
     live = jnp.arange(tokens, dtype=jnp.int32) < counts[0, 0]
     masked = jnp.where(live[:, None], grads_out, jnp.zeros_like(grads_out))
     d_full = scale * jnp.dot(
-        masked, lax.all_gather(matrix, DP, axis=0, tiled=True).T, preferred_element_type=jnp.float32
+        masked,
+        jnp.concatenate(
+            lax.all_to_all(jnp.stack([matrix] * lax.axis_size(DP)), DP, 0, 0), axis=0
+        ).T,
+        preferred_element_type=jnp.float32,
     )
     d_hid = d_full.astype(jnp.bfloat16)
     full_term = scale * jnp.dot(acts.T, masked, preferred_element_type=jnp.float32)

time: 302 us -> 343 us (1.14)
  waiting for transfers between devices: 232 us -> 260 us
  starting transfers between devices: 0.17 us -> 8.82 us
  local copies, waits for them, and re-layouts: 11.6 us -> 15.5 us
    unnamed x5 -> x4, waiting for transfers between devices: 42.8 us -> 116 us
    all_gather x1 -> x0, waiting for transfers between devices: 54.5 us -> none  [on_device(): lax.all_gather(matrix, DP, axis=0, tiled=True)]
    reduce_scatter x2, waiting for transfers between devices: 135 us -> 144 us  [summed_rows(): nearer = lax.psum_scatter(array, axes[0], scatter_dimension=dim, tiled=True)]
    all_to_all x0 -> x1, starting transfers between devices: none -> 8.7 us  [on_device(): lax.all_to_all(jnp.stack([matrix] * lax.axis_size(DP)), DP, 0, 0)]
    another operation x0 -> x1, local copies, waits for them, and re-layouts: none -> 3.9 us  [on_device(): jnp.stack([matrix] * lax.axis_size(DP))]
  transfers between devices with their start and end apart: 4 -> 4, of which waited for: 3 -> 3; matrix products, arithmetic and copies ran while one was open for 4% -> 5% of each run, Pallas kernels for 0% -> 0%
where the time goes in v1:
time: 343 us; the launch traced here: 342 us
  waiting for transfers between devices  260 us (76%)
  matrix products  27.6 us (8%)
  local copies, waits for them, and re-layouts  15.5 us (5%)
  between operations  14.7 us (4%)
  blocking collectives  9.92 us (3%)
  starting transfers between devices  8.82 us (3%)
  other arithmetic  5.79 us (2%)
    reduce_scatter x2, waiting for transfers between devices, summed_rows(): nearer = lax.psum_scatter(array, axes[0], scatter_dimension=dim, tiled=True)  144 us
    unnamed x4, waiting for transfers between devices  116 us
    dot_general x1, matrix products, on_device(): jnp.dot(acts.T, masked, preferred_element_type=jnp.float32)  14.4 us
    dot_general x1, matrix products, on_device(): jnp.dot(masked, jnp.concatenate(lax.all_to_all(jnp.stack([matrix] * lax.a...  13.2 us
    all_to_all x1, starting transfers between devices, on_device(): lax.all_to_all(jnp.stack([matrix] * lax.axis_size(DP)), DP, 0, 0)  8.7 us
  transfers between devices with their start and end apart: 4, of which 3 were waited for; matrix products, arithmetic and copies ran while one was open for 5% of the time, Pallas kernels for 0%

profile of v1, /device:TPU:1, one launch (start us, length us, event | category | flops | bytes accessed | tf_op | source)
XLA Modules:
  0.0 342.5 jit_solution(6336566225699425201)
XLA Ops:
  7.2 0.0 copy-start
  7.2 0.0 reduce-scatter.8.cloned.1.call-start
  8.0 0.8 copy-done
  8.8 14.4 %multiply_bitcast_fusion = f32[1024,3584]{0,1:T(8,128)} fusion(bf16[1,1024,3584]{2,1,0:T(8,128)(2,1)} %param.9, pred[1024]{0:T(1024)(128)(4,1)S(1)} %iota_compare_fusion, bf16[1,1024,1024]{2,1,0:T(8,128)(2,1)S(1)} %copy-done), kind=kOutput, calls=%fused_computation.1 | convolution fusion | flops 7523532800 | bytes 24118272 | tf_op jit(solution)/shard_map/dot_general | solution.py:43
  23.2 0.0 reduce-scatter.8.cloned.1.call-update
  23.2 0.0 copy-start.1
  23.2 0.0 reduce-scatter.10.cloned.1.call-start
  23.2 135.1 %reduce-scatter.8.cloned.1.call-done = f32[256,3584]{0,1:T(8,128)} async-done(((f32[1024,3584]{0,1:T(8,128)}), f32[256,3584]{0,1:T(8,128)}) %reduce-scatter.8.cloned.1.call-update) | async-done | bytes 3670032 | tf_op jit(solution)/shard_map/reduce_scatter | solution.py:21
  158.3 5.1 %copy.62 = f32[256,3584]{1,0:T(8,128)} copy(f32[256,3584]{0,1:T(8,128)} %reduce-scatter.8.cloned.1.call-done) | data formatting | bytes 7340032
  163.4 0.0 reduce-scatter.10.cloned.1.call-update
  163.5 0.0 copy-done.1
  163.5 3.9 %stack.3 = bf16[64,16,3584]{2,1,0:T(8,128)(2,1)} broadcast(bf16[16,3584]{1,0:T(8,128)(2,1)S(1)} %bitcast.53), dimensions={1,2} | broadcast | bytes 7454720 | tf_op jit(solution)/shard_map/stack | solution.py:38
  167.4 0.0 copy-start.4
  167.4 8.7 %all-to-all-start = ((bf16[64,16,3584]{2,1,0:T(8,128)(2,1)}), bf16[64,16,3584]{2,1,0:T(8,128)(2,1)}, u32[]{:S(2)}, u32[]{:S(2)}) async-start(bf16[64,16,3584]{2,1,0:T(8,128)(2,1)} %stack.3), calls=%async_computation | async-start | bytes 14680064 | tf_op jit(solution)/shard_map/all_to_all | solution.py:38
  176.1 0.0 reduce-scatter.12.cloned.1.call-start
  176.1 0.0 copy-done.4
  176.2 0.1 copy.59
  176.2 0.1 reshape.64
  176.3 115.8 %reduce-scatter.10.cloned.1.call-done = f32[64,3584]{1,0:T(8,128)} async-done(((f32[256,3584]{1,0:T(8,128)}), f32[64,3584]{1,0:T(8,128)}) %reduce-scatter.10.cloned.1.call-update) | async-done | bytes 917520
  292.2 0.0 reduce-scatter.12.cloned.1.call-update
  292.2 0.0 all-to-all-done
  292.2 0.0 copy-start.2
  292.2 0.0 copy-start.3
  292.3 13.2 %fusion.3 = bf16[1,1024,1024]{2,1,0:T(8,128)(2,1)} fusion(bf16[1024,3584]{1,0:T(8,128)(2,1)} %bitcast.3, bf16[1,1024,3584]{2,1,0:T(8,128)(2,1)} %param.9, pred[1024]{0:T(1024)(128)(4,1)S(1)} %iota_compare_fusion), kind=kOutput, calls=%fused_computation.7 | convolution fusion | flops 7521959936 | bytes 16778240 | tf_op jit(solution)/shard_map/dot_general | solution.py:35
  305.5 9.2 %reduce-scatter.12.cloned.1.call-done = f32[16,3584]{1,0:T(8,128)} async-done(((f32[64,3584]{1,0:T(8,128)}), f32[16,3584]{1,0:T(8,128)}) %reduce-scatter.12.cloned.1.call-update) | async-done | bytes 229392 | tf_op jit(solution)/shard_map/reduce_scatter | solution.py:21
  314.7 0.0 copy-done.2
  314.7 0.0 copy-done.3
  314.7 1.9 fusion.9
  316.6 0.1 all_to_all.19
  316.6 0.5 broadcast.58
  317.2 1.4 reduce
  318.6 0.1 reshape.76
  318.7 5.8 %all_to_all.23 = bf16[2,2,14336]{2,1,0:T(2,128)(2,1)S(1)} all-to-all(bf16[2,2,14336]{2,1,0:T(2,128)(2,1)S(1)} %reshape.76), channel_id=1, replica_groups=mesh['dp_0'=4,'dp_1'=4,'dp_2'=4,'expert'=2] {'expert'}, dimensions={0} | all-to-all | bytes 229376 | tf_op jit(solution)/shard_map/all_to_all | solution.py:53
  324.5 0.1 reshape.77
  324.6 0.2 copy.69
  324.8 0.8 gather_fusion
  325.7 0.3 reshape.63
  326.0 0.6 copy_select_fusion
  326.6 4.1 %all_to_all.24 = bf16[4,2,28672]{2,0,1:T(4,128)(2,1)S(1)} all-to-all(bf16[4,2,28672]{2,0,1:T(4,128)(2,1)S(1)} %copy_select_fusion), channel_id=1, replica_groups=mesh['dp_0'=4,'dp_1'=4,'dp_2'=4,'expert'=2] {'expert'}, dimensions={1} | all-to-all | bytes 917504 | tf_op jit(solution)/shard_map/all_to_all | solution.py:55
  330.7 1.4 copy.61
  332.1 2.0 reshape.61
  334.1 1.9 add_convert_fusion
  (4 shorter events, 0.0 us)
Async XLA Ops:
  7.2 1.6 copy-start
  7.2 151.1 %reduce-scatter.8.cloned.1.call-start = ((), (), s32[]{:S(2)}) async-start(), calls=%async_computation.6 | async-start | bytes 18350080 | tf_op jit(solution)/shard_map/reduce_scatter | solution.py:21
  23.2 140.3 %copy-start.1 = (bf16[1,16,3584]{2,1,0:T(8,128)(2,1)S(1)}, bf16[1,16,3584]{2,1,0:T(8,128)(2,1)}, u32[]{:S(2)}) copy-start(bf16[1,16,3584]{2,1,0:T(8,128)(2,1)} %param.12) | copy-start | bytes 344068
  23.2 269.0 %reduce-scatter.10.cloned.1.call-start = ((), (), s32[]{:S(2)}) async-start(), calls=%async_computation.7 | async-start | bytes 4587520
  167.4 8.8 %copy-start.4 = (s32[2,4]{1,0:T(2,128)S(1)}, s32[2,4]{1,0:T(2,128)}, u32[]{:S(2)}) copy-start(s32[2,4]{1,0:T(2,128)} %param.11) | copy-start | bytes 100
  167.4 124.9 %all-to-all-start = ((bf16[64,16,3584]{2,1,0:T(8,128)(2,1)}), bf16[64,16,3584]{2,1,0:T(8,128)(2,1)}, u32[]{:S(2)}, u32[]{:S(2)}) async-start(bf16[64,16,3584]{2,1,0:T(8,128)(2,1)} %stack.3), calls=%async_computation | async-start | bytes 14680064 | tf_op jit(solution)/shard_map/all_to_all | solution.py:38
  176.1 138.6 %reduce-scatter.12.cloned.1.call-start = ((), (), s32[]{:S(2)}) async-start(), calls=%async_computation.8 | async-start | bytes 1146880 | tf_op jit(solution)/shard_map/reduce_scatter | solution.py:21
  292.2 22.5 %copy-start.2 = (f32[1,16,3584]{2,1,0:T(8,128)S(1)}, f32[1,16,3584]{2,1,0:T(8,128)}, u32[]{:S(2)}) copy-start(f32[1,16,3584]{2,1,0:T(8,128)} %param.14) | copy-start | bytes 688132
  292.2 22.5 %copy-start.3 = (f32[1,16,3584]{2,1,0:T(8,128)S(1)}, f32[1,16,3584]{2,1,0:T(8,128)}, u32[]{:S(2)}) copy-start(f32[1,16,3584]{2,1,0:T(8,128)} %param.13) | copy-start | bytes 688132
Sparse Core Ops, SparseCore 0:
  23.3 134.9 reduce-scatter.7
  163.6 128.5 reduce-scatter.9
  294.6 20.0 reduce-scatter.11
